TPU v7x, 1024 devices: a whole 8x8x8 slice. The times are simulated.
1024 devices in a mesh: rep: 32 (over y, z_hi), fsdp: 32 (over x, z_lo, core).
Axes of the slice: x: 8, y: 8, z: 8 (z_hi: 4, z_lo: 2; z = z_hi * 2 + z_lo), core: 2. Of those that a mesh axis runs over, the one named last changes fastest.
Arguments:
- tokens: bfloat16 [32, 512, 8192], P('rep', None, 'fsdp'), may hold values from -6 to 6
- targets: bfloat16 [32, 512, 1024], P('rep', 'fsdp'), may hold values from -6 to 6
- inner_weights: float32 [32, 8192, 1024], P('rep', 'fsdp'), may hold values from -6 to 6
- outer_weights: float32 [8192, 1024], P('fsdp'), may hold values from -6 to 6
- outer_momentum: float32 [8192, 1024], P('fsdp'), may hold values from -3 to 3
- replica_weights: bfloat16 [32, 8192, 1024], P('rep', 'fsdp'), may hold values from -6 to 6
Outputs:
- new_inner: float32 [32, 8192, 1024], P('rep', 'fsdp')
- new_outer: float32 [8192, 1024], P('fsdp')
- new_moment: float32 [8192, 1024], P('fsdp')
- merged: bfloat16 [32, 8192, 1024], P('rep', 'fsdp')
All inputs are finite; a program needn't handle non-finite values.
Results may differ from a plain program's by a relative error of at most 0.005.
Values may be sent and summed in bfloat16 or wider, within the bound.
A program may use at most 32 MiB of HBM per device.

v0:
```python
import jax
import jax.numpy as jnp
from jax import lax
from jax.sharding import PartitionSpec as P

D = 8192
INNER = 2


inner_rate = 0.5
momentum_coef = 0.9
outer_rate = 0.7
merge_keep = 0.5


def outer_update(outer_part, moment_part, outer_delta):
    new_moment = momentum_coef * moment_part + outer_delta
    new_outer = outer_part - outer_rate * (outer_delta + momentum_coef * new_moment)
    return (new_outer, new_moment)


def outer_sync(outer_weights, outer_momentum, replica_weights):
    replica_rows = replica_weights[0].astype(jnp.float32)
    replica_term = outer_weights - replica_rows
    replica_count = lax.axis_size("rep")
    pseudo_sum = lax.psum(replica_term, "rep")
    new_outer, new_moment = outer_update(outer_weights, outer_momentum, pseudo_sum / replica_count)
    mixed = merge_keep * replica_rows + (1.0 - merge_keep) * new_outer
    merged = mixed.astype(jnp.bfloat16)[None]
    return (new_outer, new_moment, merged)


def inner_run(tokens, targets, inner_weights):
    token_cols = tokens[0]
    target_rows = targets[0]
    weights_now = inner_weights[0]
    weight_scale = D ** (-0.5)
    for inner_turn in range(INNER):
        weights_half = weights_now.astype(jnp.bfloat16)
        predicted = (
            lax.psum_scatter(
                jnp.dot(token_cols, weights_half, preferred_element_type=jnp.float32).astype(
                    jnp.bfloat16
                ),
                "fsdp",
                scatter_dimension=0,
                tiled=True,
            ).astype(jnp.float32)
            * weight_scale
        )
        errors = (predicted - target_rows.astype(jnp.float32)).astype(jnp.bfloat16)
        gradient = (
            lax.dot_general(
                token_cols,
                lax.all_gather(errors, "fsdp", axis=0, tiled=True),
                (((0,), (0,)), ((), ())),
                preferred_element_type=jnp.float32,
            )
            * weight_scale
        )
        weights_now = weights_now - inner_rate * gradient
    return weights_now[None]


def local(tokens, targets, inner_weights, outer_weights, outer_momentum, replica_weights):
    new_outer, new_moment, merged = outer_sync(outer_weights, outer_momentum, replica_weights)
    new_inner = inner_run(tokens, targets, inner_weights)
    return (new_inner, new_outer, new_moment, merged)


def solution(mesh):
    placed = (
        P("rep", None, "fsdp"),
        P("rep", "fsdp", None),
        P("rep", "fsdp", None),
        P("fsdp", None),
        P("fsdp", None),
        P("rep", "fsdp", None),
    )
    return jax.shard_map(
        local,
        mesh=mesh,
        in_specs=placed,
        out_specs=(
            P("rep", "fsdp", None),
            P("fsdp", None),
            P("fsdp", None),
            P("rep", "fsdp", None),
        ),
        check_vma=False,
    )
```

profile of v0, /device:TPU:6, one launch (start us, length us, event | category | flops | bytes accessed | tf_op | source)
XLA Modules:
  0.0 570.3 jit_solution(8928976461511804618)
XLA Ops:
  8.0 0.0 copy-start
  8.0 0.0 reduce-scatter.3.cloned.1.call-start
  8.1 0.9 copy-done
  9.0 0.0 copy-start.4
  9.0 2.6 convolution_convert_fusion.1
  11.6 0.0 copy-start.1
  11.6 0.0 reduce-scatter.3.cloned.1.call-update
  11.6 0.0 all-gather.3.cloned.1.call-start
  11.7 129.5 %reduce-scatter.3.cloned.1.call-done = bf16[16,1024]{1,0:T(8,128)(2,1)} async-done(((bf16[512,1024]{1,0:T(8,128)(2,1)}), bf16[16,1024]{1,0:T(8,128)(2,1)}) %reduce-scatter.3.cloned.1.call-update) | async-done | bytes 32784 | tf_op jit(solution)/shard_map/reduce_scatter | solution.py:41
  141.2 0.0 copy-done.4
  141.2 1.4 fusion.16
  142.6 0.0 all-gather.3.cloned.1.call-update
  142.6 0.0 reduce-scatter.5.cloned.1.call-start
  142.7 0.0 copy-done.1
  142.7 0.3 copy.10
  143.0 74.2 %all-gather.3.cloned.1.call-done = bf16[512,1024]{1,0:T(8,128)(2,1)} async-done(((bf16[16,1024]{1,0:T(8,128)(2,1)}), bf16[512,1024]{1,0:T(8,128)(2,1)}) %all-gather.3.cloned.1.call-update) | async-done | bytes 1048592 | tf_op jit(solution)/shard_map/all_gather | solution.py:55
  217.2 1.7 fusion.5
  218.9 0.0 copy-start.3
  218.9 1.4 fusion
  220.4 0.0 copy-start.2
  220.4 0.0 reduce-scatter.5.cloned.1.call-update
  220.4 0.0 all-reduce.2.cloned.1.call-start
  220.5 0.0 copy-done.3
  220.5 1.1 copy-done.2
  221.6 1.1 convert_subtract_fusion
  222.7 0.0 all-reduce.2.cloned.1.call-update
  222.7 0.0 all-gather.5.cloned.1.call-start
  222.8 118.8 %reduce-scatter.5.cloned.1.call-done = bf16[16,1024]{1,0:T(8,128)(2,1)} async-done(((bf16[512,1024]{1,0:T(8,128)(2,1)}), bf16[16,1024]{1,0:T(8,128)(2,1)}) %reduce-scatter.5.cloned.1.call-update) | async-done | bytes 32784 | tf_op jit(solution)/shard_map/reduce_scatter | solution.py:41
  341.6 1.4 fusion.17
  343.0 0.0 all-gather.5.cloned.1.call-update
  343.0 213.6 %all-reduce.2.cloned.1.call-done = f32[256,1024]{1,0:T(8,128)} async-done(((f32[256,1024]{1,0:T(8,128)}), f32[256,1024]{1,0:T(8,128)}) %all-reduce.2.cloned.1.call-update) | async-done | bytes 1048592 | tf_op jit(solution)/shard_map/psum | solution.py:26
  556.6 3.5 fusion.8
  560.1 0.0 all-gather.5.cloned.1.call-done
  560.1 1.7 fusion.3
  561.8 1.3 copy.11
Async XLA Ops:
  8.0 1.0 copy-start
  8.0 133.2 %reduce-scatter.3.cloned.1.call-start = ((), (), s32[]{:S(2)}) async-start(), calls=%async_computation.2 | async-start | bytes 1081344 | tf_op jit(solution)/shard_map/reduce_scatter | solution.py:41
  9.0 132.2 %copy-start.4 = (bf16[1,16,1024]{2,1,0:T(8,128)(2,1)S(1)}, bf16[1,16,1024]{2,1,0:T(8,128)(2,1)}, u32[]{:S(2)}) copy-start(bf16[1,16,1024]{2,1,0:T(8,128)(2,1)} %param.7) | copy-start | bytes 98308
  11.6 131.1 %copy-start.1 = (f32[1,256,1024]{2,1,0:T(8,128)S(1)}, f32[1,256,1024]{2,1,0:T(8,128)}, u32[]{:S(2)}) copy-start(f32[1,256,1024]{2,1,0:T(8,128)} %param.8) | copy-start | bytes 3145732
  11.6 205.6 %all-gather.3.cloned.1.call-start = ((), (), s32[]{:S(2)}) async-start(), calls=%async_computation.3 | async-start | bytes 1081344 | tf_op jit(solution)/shard_map/all_gather | solution.py:55
  142.6 199.0 %reduce-scatter.5.cloned.1.call-start = ((), (), s32[]{:S(2)}) async-start(), calls=%async_computation.4 | async-start | bytes 1081344 | tf_op jit(solution)/shard_map/reduce_scatter | solution.py:41
  218.9 1.5 copy-start.3
  220.4 1.2 copy-start.2
  220.4 336.2 %all-reduce.2.cloned.1.call-start = ((), (), s32[]{:S(2)}) async-start(), calls=%async_computation.6 | async-start | bytes 2097152 | tf_op jit(solution)/shard_map/psum | solution.py:26
  222.7 337.4 %all-gather.5.cloned.1.call-start = ((), (), s32[]{:S(2)}) async-start(), calls=%async_computation.5 | async-start | bytes 1081344 | tf_op jit(solution)/shard_map/all_gather | solution.py:55
Sparse Core Ops, SparseCore 0:
  12.8 128.3 reduce-scatter.2
  144.5 72.6 all-gather.2
  221.2 120.4 reduce-scatter.4
  344.8 72.4 all-gather.4
Sparse Core Ops, SparseCore 1:
  225.0 331.6 all-reduce.1
where the time goes:
time: 571 us; the launch traced here: 570 us
  waiting for transfers between devices  536 us (94%)
  between operations  15.3 us (3%)
  matrix products  7.47 us (1%)
  other arithmetic  7.38 us (1%)
    reduce_scatter x2, waiting for transfers between devices, inner_run(): lax.psum_scatter(jnp.dot(token_cols, weights_half, preferred_element_type...  248 us
    psum x1, waiting for transfers between devices, outer_sync(): pseudo_sum = lax.psum(replica_term, 'rep')  214 us
    all_gather x2, waiting for transfers between devices, inner_run(): lax.all_gather(errors, 'fsdp', axis=0, tiled=True)  74.2 us
  transfers between devices with their start and end apart: 5, of which 4 were waited for; matrix products, arithmetic and copies ran while one was open for 1% of the time, Pallas kernels for 0%

commit v1 on v0

v1 whole, which is shorter than its diff:
```python
import functools

import jax
import jax.numpy as jnp
from jax import lax
from jax.experimental import pallas as pl
from jax.experimental.pallas import tpu as pltpu
from jax.sharding import PartitionSpec as P

D = 8192
REPS = 32
inner_rate = 0.5
momentum_coef = 0.9
outer_rate = 0.7
merge_keep = 0.5

NX, NZ, NC = 8, 2, 2
NY, NH = 8, 4
MESH = pl.DeviceIdType.MESH
F32, BF16 = jnp.float32, jnp.bfloat16


class Copies:
    def __init__(self, send_sems, recv_sems):
        self.send_sems, self.recv_sems = send_sems, recv_sems
        self.made = {}

    def start(self, name, src, dst, device):
        slot = len(self.made)
        assert slot < self.send_sems.shape[0]
        copy = pltpu.make_async_remote_copy(
            src_ref=src,
            dst_ref=dst,
            send_sem=self.send_sems.at[slot],
            recv_sem=self.recv_sems.at[slot],
            device_id=device,
            device_id_type=MESH,
        )
        copy.start()
        self.made[name] = copy

    def arrived(self, name):
        self.made[name].wait_recv()

    def drain(self):
        for copy in self.made.values():
            copy.wait_send()


def hops(direction, block):
    return 4 if (direction == 0) == (block == 0) else 3


def comm_kernel(inner, outer, weight_scale, x_hbm, w_hbm, t_hbm, o_hbm, r_hbm,
                e_out, k_out, d_out,
                xv, wv, tv, ov, rv, qown, qoth, qpar, rx, sx, zs, zr, ek,
                ry, sy, ysum, hr, dv,
                load_sems, store_sems, send_sems, recv_sems):
    rep, fsdp = lax.axis_index("rep"), lax.axis_index("fsdp")
    x, z, c = fsdp // 4, (fsdp // 2) % 2, fsdp % 2
    y, h = rep // 4, rep % 4
    cols = w_hbm.shape[1]
    toks = k_out.shape[-1]
    wide = cols + toks
    half = ov.shape[2] // 2
    quarter = ov.shape[2] // 4

    def at_x(k):
        return lax.rem(x + k + NX, NX)

    def at_y(k):
        return lax.rem(y + k + NY, NY)

    def to_x(k):
        return {"fsdp": at_x(k) * 4 + z * 2 + c}

    def to_y(k):
        return {"rep": at_y(k) * 4 + h}

    def to_h(k):
        return {"rep": y * 4 + lax.rem(h + k, NH)}

    core = {"fsdp": x * 4 + z * 2 + 1 - c}
    zlo = {"fsdp": x * 4 + (1 - z) * 2 + c}

    loads = {}
    for slot, (name, src, dst) in enumerate((("x", x_hbm, xv), ("w", w_hbm, wv), ("o", o_hbm, ov), ("r", r_hbm, rv), ("t", t_hbm, tv))):
        loads[name] = pltpu.make_async_copy(src, dst, load_sems.at[slot])
        loads[name].start()

    barrier = pltpu.get_barrier_semaphore()
    peers = []
    if inner:
        peers += [core, zlo, to_x(1), to_x(-1)]
    if outer:
        peers += [to_y(1), to_y(-1), to_h(1), to_h(2), to_h(3)]
    for peer in peers:
        pl.semaphore_signal(barrier, inc=1, device_id=peer, device_id_type=MESH)

    net = Copies(send_sems, recv_sems)

    def rows_of(core_index):
        return xv[:, :, core_index].reshape(NX * NZ * 16, xv.shape[-1])

    def partial(rows, start, width):
        if start < cols:
            out = jnp.dot(rows, wv[:, start:start + width].astype(BF16), preferred_element_type=F32)
        else:
            every = xv[...].reshape(toks, xv.shape[-1])
            out = lax.dot_general(rows, every, (((1,), (1,)), ((), ())), preferred_element_type=F32)
        return out.reshape(NX, NZ, 16, width)

    tiles = [(start, cols // 2) for start in (0, cols // 2)] + [(cols, toks)]

    loads["x"].wait()
    loads["w"].wait()
    if inner:
        rows = rows_of(1 - c)
        for start, width in tiles:
            qoth[:, :, :, start:start + width] = partial(rows, start, width).astype(BF16)

    pl.semaphore_wait(barrier, len(peers))

    if inner:
        for k in (4, 3, 5, 2, 6, 1, 7, 0):
            net.start(("core", k), qoth.at[at_x(k)], qpar.at[at_x(k)], core)

    def y_own(k, block):
        at = slice(block * half, (block + 1) * half)
        return ov[at_y(k), :, at] - rv[at_y(k), :, at].astype(F32)

    def y_send(direction, block, j):
        step = 1 if direction == 0 else -1
        value = y_own(step * j, block)
        if j < hops(direction, block):
            net.arrived(("ry", direction, block, j + 1))
            value = value + ry[direction, block, j].astype(F32)
        sy[direction, block, j - 1] = value.astype(BF16)
        net.start(("ry", direction, block, j), sy.at[direction, block, j - 1], ry.at[direction, block, j - 1], to_y(step))

    def y_final(block):
        for direction in (0, 1):
            net.arrived(("ry", direction, block, 1))
        at = slice(block * half, (block + 1) * half)
        ysum[:, at] = y_own(0, block) + (ry[0, block, 0].astype(F32) + ry[1, block, 0].astype(F32))

    merged = set()

    def merge(k):
        k = k % NX
        if k not in merged:
            merged.add(k)
            net.arrived(("core", k))
            qown[at_x(k)] = qown[at_x(k)] + qpar[at_x(k)].astype(F32)

    def zz(block):
        return 1 - z if block == 0 else z

    def x_send(direction, block, j):
        step = 1 if direction == 0 else -1
        merge(step * j)
        value = qown[at_x(step * j), zz(block)]
        if j < hops(direction, block):
            net.arrived(("rx", direction, block, j + 1))
            value = value + rx[direction, block, j].astype(F32)
        sx[direction, block, j - 1] = value.astype(BF16)
        net.start(("rx", direction, block, j), sx.at[direction, block, j - 1], rx.at[direction, block, j - 1], to_x(step))

    def x_final(block):
        merge(0)
        for direction in (0, 1):
            net.arrived(("rx", direction, block, 1))
        return qown[x, zz(block)] + (rx[0, block, 0].astype(F32) + rx[1, block, 0].astype(F32))

    order = ((0, 0), (1, 1), (0, 1), (1, 0))

    if outer:
        loads["o"].wait()
        loads["r"].wait()
        for direction, block in order:
            y_send(direction, block, hops(direction, block))
    if inner:
        rows = rows_of(c)
        for start, width in tiles:
            qown[:, :, :, start:start + width] = partial(rows, start, width)
        for direction, block in order:
            x_send(direction, block, hops(direction, block))
    for j in (3, 2, 1):
        for ring, send in ((outer, y_send), (inner, x_send)):
            if ring:
                for direction, block in order:
                    if j < hops(direction, block):
                        send(direction, block, j)

    if outer:
        y_final(0)
        y_final(1)
        for k in (2, 1, 3):
            at = pl.ds(pl.multiple_of(lax.rem(h + k, NH) * quarter, 128), quarter)
            net.start(("hr", k), ysum.at[:, at], hr.at[k - 1], to_h(k))
    if inner:
        zs[...] = x_final(0).astype(BF16)
        net.start("zr", zs, zr, zlo)
        mine = x_final(1)
        loads["t"].wait()
        net.arrived("zr")
        total = mine + zr[...].astype(F32)
        ek[x, z, c, :, 0:cols] = (total[:, 0:cols] * weight_scale - tv[...].astype(F32)).astype(BF16)
        ek[x, z, c, :, cols:wide] = total[:, cols:wide].astype(BF16)

    def g_slot(k, block):
        return ek.at[at_x(k), z if block == 0 else 1 - z, c]

    def g_pass(direction, block, i):
        step = 1 if direction == 0 else -1
        slot = g_slot(-step * i, block)
        if i > 0:
            net.arrived(("gx", direction, block, i))
            net.start(("gc", direction, block, i), slot, slot, core)
        if i < hops(direction, block):
            net.start(("gx", direction, block, i + 1), slot, slot, to_x(step))

    def g_own(block):
        slot = g_slot(0, block)
        for direction in (0, 1):
            g_pass(direction, block, 0)
        net.start(("gc", block), slot, slot, core)

    def d_slot(k, block):
        return dv.at[at_y(k), :, block * half:(block + 1) * half]

    def d_pass(direction, block, i):
        step = 1 if direction == 0 else -1
        slot = d_slot(-step * i, block)
        if i > 0:
            net.arrived(("gy", direction, block, i))
        if i < hops(direction, block):
            net.start(("gy", direction, block, i + 1), slot, slot, to_y(step))

    def g_hop(block, i):
        if inner:
            for direction in (0, 1):
                if i <= hops(direction, block):
                    g_pass(direction, block, i)

    def d_hop(i):
        if outer:
            for direction, block in order:
                if i <= hops(direction, block):
                    d_pass(direction, block, i)

    if inner:
        slot = g_slot(0, 0)
        net.start("gz", slot, slot, zlo)
        g_own(0)
    if outer:
        own = pl.ds(pl.multiple_of(h * quarter, 128), quarter)
        value = ysum[:, own]
        for k in (1, 3, 2):
            net.arrived(("hr", k))
            value = value + hr[k - 1]
        dv[y, :, own] = value / REPS
        for k in (2, 1, 3):
            net.start(("gh", k), dv.at[y, :, own], dv.at[y, :, own], to_h(k))
    g_hop(0, 1)
    if inner:
        net.arrived("gz")
        g_own(1)
    g_hop(0, 2)
    g_hop(1, 1)
    if outer:
        for k in (1, 3, 2):
            net.arrived(("gh", k))
    d_hop(0)
    g_hop(0, 3)
    g_hop(1, 2)
    d_hop(1)
    g_hop(0, 4)
    g_hop(1, 3)
    d_hop(2)
    g_hop(1, 4)
    d_hop(3)
    if inner:
        for name in list(net.made):
            if name[0] == "gc":
                net.arrived(name)
    stores = []
    if inner:
        stores.append(pltpu.make_async_copy(ek.at[:, :, :, :, 0:cols], e_out, store_sems.at[0]))
        stores.append(pltpu.make_async_copy(ek.at[:, :, :, :, cols:wide], k_out, store_sems.at[1]))
        for store in stores:
            store.start()
    d_hop(4)
    if outer:
        stores.append(pltpu.make_async_copy(dv, d_out, store_sems.at[2]))
        stores[-1].start()
    for store in stores:
        store.wait()
    if not inner:
        loads["t"].wait()
    if not outer:
        loads["o"].wait()
        loads["r"].wait()
    net.drain()


def exchange(tokens, targets, weights, outer_weights, replica, inner=True, outer=True):
    toks, feats = tokens.shape
    cols = weights.shape[1]
    wide = cols + toks
    o_cols = outer_weights.shape[1]
    y_rows = outer_weights.shape[0] // NY
    weight_scale = D ** (-0.5)
    hbm = pl.BlockSpec(memory_space=pl.ANY)
    copies = 88
    e, k, delta = pl.pallas_call(
        functools.partial(comm_kernel, inner, outer, weight_scale),
        out_shape=(
            jax.ShapeDtypeStruct((NX, NZ, NC, 16, cols), BF16),
            jax.ShapeDtypeStruct((NX, NZ, NC, 16, toks), BF16),
            jax.ShapeDtypeStruct((NY, y_rows, o_cols), F32),
        ),
        in_specs=[hbm] * 5,
        out_specs=(hbm,) * 3,
        scratch_shapes=[
            pltpu.VMEM((NX, NZ, NC, 16, feats), BF16),
            pltpu.VMEM((feats, cols), F32),
            pltpu.VMEM((16, cols), BF16),
            pltpu.VMEM((NY, y_rows, o_cols), F32),
            pltpu.VMEM((NY, y_rows, o_cols), BF16),
            pltpu.VMEM((NX, NZ, 16, wide), F32),
            pltpu.VMEM((NX, NZ, 16, wide), BF16),
            pltpu.VMEM((NX, NZ, 16, wide), BF16),
            pltpu.VMEM((2, 2, 4, 16, wide), BF16),
            pltpu.VMEM((2, 2, 4, 16, wide), BF16),
            pltpu.VMEM((16, wide), BF16),
            pltpu.VMEM((16, wide), BF16),
            pltpu.VMEM((NX, NZ, NC, 16, wide), BF16),
            pltpu.VMEM((2, 2, 4, y_rows, o_cols // 2), BF16),
            pltpu.VMEM((2, 2, 4, y_rows, o_cols // 2), BF16),
            pltpu.VMEM((y_rows, o_cols), F32),
            pltpu.VMEM((3, y_rows, o_cols // 4), F32),
            pltpu.VMEM((NY, y_rows, o_cols), F32),
            pltpu.SemaphoreType.DMA((5,)),
            pltpu.SemaphoreType.DMA((3,)),
            pltpu.SemaphoreType.DMA((copies,)),
            pltpu.SemaphoreType.DMA((copies,)),
        ],
        compiler_params=pltpu.CompilerParams(collective_id=0, has_side_effects=True),
    )(
        tokens.reshape(NX, NZ, NC, 16, feats),
        weights,
        targets,
        outer_weights.reshape(NY, y_rows, o_cols),
        replica.reshape(NY, y_rows, o_cols),
    )
    return e.reshape(toks, cols), k.reshape(toks, toks), delta.reshape(outer_weights.shape)


def local(tokens, targets, inner_weights, outer_weights, outer_momentum, replica_weights):
    token_cols, replica = tokens[0], replica_weights[0]
    errors, products, outer_delta = exchange(token_cols, targets[0], inner_weights[0], outer_weights, replica)

    new_moment = momentum_coef * outer_momentum + outer_delta
    new_outer = outer_weights - outer_rate * (outer_delta + momentum_coef * new_moment)
    mixed = merge_keep * replica.astype(F32) + (1.0 - merge_keep) * new_outer

    turned = jnp.dot(products, token_cols, preferred_element_type=F32)
    both = (2.0 * token_cols.astype(F32) - (inner_rate / D) * turned).astype(BF16)
    gradient = lax.dot_general(both, errors, (((0,), (0,)), ((), ())), preferred_element_type=F32)
    new_inner = inner_weights[0] - (inner_rate * D ** (-0.5)) * gradient
    return (new_inner[None], new_outer, new_moment, mixed.astype(BF16)[None])


def solution(mesh):
    placed = (
        P("rep", None, "fsdp"),
        P("rep", "fsdp", None),
        P("rep", "fsdp", None),
        P("fsdp", None),
        P("fsdp", None),
        P("rep", "fsdp", None),
    )
    return jax.shard_map(
        local,
        mesh=mesh,
        in_specs=placed,
        out_specs=(
            P("rep", "fsdp", None),
            P("fsdp", None),
            P("fsdp", None),
            P("rep", "fsdp", None),
        ),
        check_vma=False,
    )
```

time: 571 us -> 74.2 us (0.13)
  the two profiles are of different devices: /device:TPU:6 before, /device:TPU:2 now
where the time goes in v1:
time: 74.2 us; the launch traced here: 74 us
  Pallas kernels  66.4 us (89%)
  other arithmetic  3.51 us (5%)
  matrix products  3.41 us (5%)
    pallas_call x1, Pallas kernels, exchange(): pl.pallas_call(functools.partial(comm_kernel, inner, outer, weight_scale)...  66.4 us
    broadcast_in_dim x1, other arithmetic, local(): return (new_inner[None], new_outer, new_moment, mixed.astype(BF16)[None])  3.51 us
    dot_general x1, matrix products, local(): lax.dot_general(both, errors, (((0,), (0,)), ((), ())), preferred_element...  3.41 us

profile of v1, /device:TPU:2, one launch (start us, length us, event | category | flops | bytes accessed | tf_op | source)
XLA Modules:
  0.0 74.0 jit_solution(1156828772711368447)
XLA Ops:
  0.6 0.0 copy-start
  0.6 0.0 copy-start.3
  0.7 66.4 %shard_map.93 = (bf16[8,2,2,16,1024]{4,3,2,1,0:T(8,128)(2,1)}, bf16[8,2,2,16,512]{4,3,2,1,0:T(8,128)(2,1)}, f32[8,32,1024]{2,1,0:T(8,128)}) custom-call(bf16[8,2,2,16,256]{4,3,2,1,0:T(8,128)(2,1)} %bitcast.37, f32[256,1024]{1,0:T(8,128)} %bitcast.33, bf16[16,1024]{1,0:T(8,128)(2,1)} %bitcast.39, f32[8,32,1024]{2,1,0:T(8,128)} %bitcast.34, ...), custom_call_target="tpu_custom_call" | custom-call | tf_op jit(solution)/shard_map/pallas_call | solution.py:316
  67.0 0.0 copy-done
  67.0 0.0 copy-done.3
  67.0 0.0 copy-start.1
  67.0 0.0 copy-start.2
  67.1 3.4 %fusion.1 = f32[1,256,1024]{2,1,0:T(8,128)} fusion(bf16[512,1024]{1,0:T(8,128)(2,1)} %bitcast.36, bf16[512,512]{1,0:T(8,128)(2,1)} %bitcast.38, bf16[1,512,256]{2,1,0:T(8,128)(2,1)S(1)} %copy-done.3, f32[1,256,1024]{2,1,0:T(8,128)S(1)} %copy-done), kind=kOutput, calls=%fused_computation.2 | convolution fusion | flops 403832832 | bytes 3932160 | tf_op jit(solution)/shard_map/dot_general | solution.py:370
  70.5 0.0 copy-done.1
  70.5 0.0 copy-done.2
  70.5 3.5 %fusion.8 = (bf16[1,256,1024]{2,1,0:T(8,128)(2,1)}, f32[256,1024]{1,0:T(8,128)}, f32[256,1024]{1,0:T(8,128)}) fusion(bf16[1,256,1024]{2,1,0:T(8,128)(2,1)S(1)} %copy-done.2, f32[256,1024]{1,0:T(8,128)S(1)} %copy-done.1, f32[8,32,1024]{2,1,0:T(8,128)} %get-tuple-element.9, f32[256,1024]{1,0:T(8,128)} %param.10), kind=kLoop, calls=%fused_computation.13 | loop fusion | flops 2621440 | bytes 6291456 | tf_op jit(solution)/shard_map/broadcast_in_dim | solution.py:372
Async XLA Ops:
  0.6 66.4 %copy-start = (f32[1,256,1024]{2,1,0:T(8,128)S(1)}, f32[1,256,1024]{2,1,0:T(8,128)}, u32[]{:S(2)}) copy-start(f32[1,256,1024]{2,1,0:T(8,128)} %param.8) | copy-start | bytes 3145732
  0.6 66.4 %copy-start.3 = (bf16[1,512,256]{2,1,0:T(8,128)(2,1)S(1)}, bf16[1,512,256]{2,1,0:T(8,128)(2,1)}, u32[]{:S(2)}) copy-start(bf16[1,512,256]{2,1,0:T(8,128)(2,1)} %param.6) | copy-start | bytes 786436
  67.0 3.4 %copy-start.1 = (f32[256,1024]{1,0:T(8,128)S(1)}, f32[256,1024]{1,0:T(8,128)}, u32[]{:S(2)}) copy-start(f32[256,1024]{1,0:T(8,128)} %param.9) | copy-start | bytes 3145732
  67.0 3.4 %copy-start.2 = (bf16[1,256,1024]{2,1,0:T(8,128)(2,1)S(1)}, bf16[1,256,1024]{2,1,0:T(8,128)(2,1)}, u32[]{:S(2)}) copy-start(bf16[1,256,1024]{2,1,0:T(8,128)(2,1)} %param.11) | copy-start | bytes 1572868

commit v2 on v1

v2 whole, which is shorter than its diff:
```python
import functools

import jax
import jax.numpy as jnp
from jax import lax
from jax.experimental import pallas as pl
from jax.experimental.pallas import tpu as pltpu
from jax.sharding import PartitionSpec as P

D = 8192
REPS = 32
inner_rate = 0.5
momentum_coef = 0.9
outer_rate = 0.7
merge_keep = 0.5

NX, NZ, NC = 8, 2, 2
NY, NH = 8, 4
MESH = pl.DeviceIdType.MESH
F32, BF16 = jnp.float32, jnp.bfloat16


class Copies:
    def __init__(self, send_sems, recv_sems):
        self.send_sems, self.recv_sems = send_sems, recv_sems
        self.made, self.guards, self.slots = {}, {}, 0

    def make(self, name, src, dst, device, recv_like=None, guard=None):
        slot = self.slots
        self.slots += 1
        assert slot < self.send_sems.shape[0]
        recv_slot = slot if recv_like is None else self.made[recv_like][1]
        copy = pltpu.make_async_remote_copy(
            src_ref=src,
            dst_ref=dst,
            send_sem=self.send_sems.at[slot],
            recv_sem=self.recv_sems.at[recv_slot],
            device_id=device,
            device_id_type=MESH,
        )
        self.made[name] = (copy, recv_slot, guard)
        return copy

    def start(self, name, src, dst, device):
        self.make(name, src, dst, device).start()

    def begin(self, name):
        self.made[name][0].start()

    def arrived(self, name):
        self.made[name][0].wait_recv()

    def drain(self):
        for copy, _, guard in self.made.values():
            if guard is None:
                copy.wait_send()
            else:
                pl.when(guard)(copy.wait_send)


def enc(value):
    return (value * jnp.abs(value) * (value * value)).astype(BF16)


def dec(coded):
    coded = coded.astype(F32)
    root = jnp.sqrt(jnp.sqrt(jnp.abs(coded)))
    return jnp.where(coded < 0.0, -root, root)


YB = 4


def hops(direction, block, blocks):
    return 4 if (direction == 0) == (block < blocks // 2) else 3


def comm_kernel(inner, outer, weight_scale, x_hbm, w_hbm, t_hbm, o_hbm, r_hbm, m_hbm,
                w_out, o_out, m_out, r_out,
                xv, xt, wv, tv, ov, rv, mv, qown, qoth, qpar, rx, sx, zs, zr, ek,
                ry, sy, ysum, us, ub, dv,
                load_sems, send_sems, recv_sems):
    rep, fsdp = lax.axis_index("rep"), lax.axis_index("fsdp")
    x, z, c = fsdp // 4, (fsdp // 2) % 2, fsdp % 2
    y, h = rep // 4, rep % 4
    feats, cols = wv.shape
    toks = xt.shape[1]
    wide = cols + toks
    ycols = ov.shape[2] // YB

    def at_x(k):
        return lax.rem(x + k + NX, NX)

    def at_y(k):
        return lax.rem(y + k + NY, NY)

    def to_x(k):
        return {"fsdp": at_x(k) * 4 + z * 2 + c}

    def to_y(k):
        return {"rep": at_y(k) * 4 + h}

    def to_h(at):
        return {"rep": y * 4 + at}

    core = {"fsdp": x * 4 + z * 2 + 1 - c}
    zlo = {"fsdp": x * 4 + (1 - z) * 2 + c}
    above, below = lax.rem(h + 1, NH), lax.rem(h + NH - 1, NH)
    first, last = h == 0, h == NH - 1

    loads = {}
    for slot, (name, src, dst) in enumerate((("o", o_hbm, ov), ("r", r_hbm, rv), ("x", x_hbm, xv), ("w", w_hbm, wv), ("t", t_hbm, tv), ("m", m_hbm, mv))):
        loads[name] = pltpu.make_async_copy(src, dst, load_sems.at[slot])
        loads[name].start()

    barrier = pltpu.get_barrier_semaphore()

    def greet(peer):
        pl.semaphore_signal(barrier, inc=1, device_id=peer, device_id_type=MESH)

    expected = 0
    if inner:
        for peer in (core, zlo, to_x(1), to_x(-1)):
            greet(peer)
        expected += 4
    if outer:
        greet(to_y(1))
        greet(to_y(-1))

        @pl.when(jnp.logical_not(last))
        def _():
            greet(to_h(above))

        @pl.when(jnp.logical_not(first))
        def _():
            greet(to_h(below))

        expected += 2 + jnp.where(last, 0, 1) + jnp.where(first, 0, 1)

    net = Copies(send_sems, recv_sems)

    def ycut(block):
        return slice(block * ycols, (block + 1) * ycols)

    def y_own(k, block):
        return ov[at_y(k), :, ycut(block)] - rv[at_y(k), :, ycut(block)].astype(F32)

    def y_send(direction, block, j):
        step = 1 if direction == 0 else -1
        value = y_own(step * j, block)
        if j < hops(direction, block, YB):
            net.arrived(("ry", direction, block, j + 1))
            value = value + dec(ry[direction, block, j])
        sy[direction, block, j - 1] = enc(value)
        net.start(("ry", direction, block, j), sy.at[direction, block, j - 1], ry.at[direction, block, j - 1], to_y(step))

    y_order = ((0, 0), (1, 2), (0, 1), (1, 3), (0, 2), (1, 0), (0, 3), (1, 1))

    def y_first():
        for direction, block in y_order:
            y_send(direction, block, hops(direction, block, YB))

    def y_round(j):
        if outer:
            for direction, block in y_order:
                if j < hops(direction, block, YB):
                    y_send(direction, block, j)

    def y_final(block):
        for direction in (0, 1):
            net.arrived(("ry", direction, block, 1))
        at = ycut(block)
        ysum[:, at] = y_own(0, block) + (dec(ry[0, block, 0]) + dec(ry[1, block, 0]))
        net.make(("up", block), us.at[:, at], ub.at[:, at], to_h(above), guard=jnp.logical_not(last))
        slot = dv.at[y, :, at]
        for target in range(NH - 1):
            net.make(("down", block, target), slot, slot, to_h(target), recv_like=("down", block, 0) if target else None, guard=last)

        @pl.when(jnp.logical_not(first))
        def _():
            net.arrived(("up", block))
            ysum[:, at] = ysum[:, at] + dec(ub[:, at])

        @pl.when(jnp.logical_not(last))
        def _():
            us[:, at] = enc(ysum[:, at])
            net.begin(("up", block))

        @pl.when(last)
        def _():
            dv[y, :, at] = enc(ysum[:, at] / REPS)
            for target in range(NH - 1):
                net.begin(("down", block, target))

    def rows_of(core_index):
        return xv[:, :, core_index].reshape(NX * NZ * 16, feats)

    def partial(rows, start, width):
        if start < cols:
            right = wv[:, start:start + width].astype(BF16)
        else:
            right = xt[...]
        return jnp.dot(rows, right, preferred_element_type=F32).reshape(NX, NZ, 16, width)

    tiles = [(start, cols // 2) for start in (0, cols // 2)] + [(cols, toks)]

    merged = set()

    def merge(k):
        k = k % NX
        if k not in merged:
            merged.add(k)
            net.arrived(("core", k))
            qown[at_x(k)] = qown[at_x(k)] + qpar[at_x(k)].astype(F32)

    def zz(block):
        return 1 - z if block == 0 else z

    def x_send(direction, block, j):
        step = 1 if direction == 0 else -1
        merge(step * j)
        value = qown[at_x(step * j), zz(block)]
        if j < hops(direction, block, 2):
            net.arrived(("rx", direction, block, j + 1))
            value = value + rx[direction, block, j].astype(F32)
        sx[direction, block, j - 1] = value.astype(BF16)
        net.start(("rx", direction, block, j), sx.at[direction, block, j - 1], rx.at[direction, block, j - 1], to_x(step))

    def x_final(block):
        merge(0)
        for direction in (0, 1):
            net.arrived(("rx", direction, block, 1))
        return qown[x, zz(block)] + (rx[0, block, 0].astype(F32) + rx[1, block, 0].astype(F32))

    x_order = ((0, 0), (1, 1), (0, 1), (1, 0))

    def x_round(j):
        if inner:
            for direction, block in x_order:
                if j < hops(direction, block, 2):
                    x_send(direction, block, j)

    def g_slot(k, block):
        return ek.at[at_x(k), z if block == 0 else 1 - z, c]

    def g_pass(direction, block, i):
        step = 1 if direction == 0 else -1
        slot = g_slot(-step * i, block)
        if i > 0:
            net.arrived(("gx", direction, block, i))
        if i < hops(direction, block, 2):
            net.start(("gx", direction, block, i + 1), slot, slot, to_x(step))
        if i > 0:
            net.start(("gc", direction, block, i), slot, slot, core)

    def g_own(block):
        slot = g_slot(0, block)
        for direction in (0, 1):
            g_pass(direction, block, 0)
        net.start(("gc", block), slot, slot, core)

    def g_hop(block, i):
        if inner:
            for direction in (0, 1):
                if i <= hops(direction, block, 2):
                    g_pass(direction, block, i)

    def d_pass(direction, block, i):
        step = 1 if direction == 0 else -1
        slot = dv.at[at_y(-step * i), :, ycut(block)]
        if i > 0:
            net.arrived(("gy", direction, block, i))
        if i < hops(direction, block, YB):
            net.start(("gy", direction, block, i + 1), slot, slot, to_y(step))

    def d_own(block):
        @pl.when(jnp.logical_not(last))
        def _():
            net.arrived(("down", block, 0))

        for direction in (0, 1):
            d_pass(direction, block, 0)

    def d_finish(k, block):
        at, row = ycut(block), at_y(k)
        delta = dec(dv[row, :, at])
        moment = momentum_coef * mv[row, :, at] + delta
        moved = ov[row, :, at] - outer_rate * (delta + momentum_coef * moment)
        m_out[row, :, at] = moment
        o_out[row, :, at] = moved
        r_out[row, :, at] = (merge_keep * rv[row, :, at].astype(F32) + (1.0 - merge_keep) * moved).astype(BF16)

    def d_hop(i):
        if outer:
            pieces = [piece for piece in y_order if i <= hops(*piece, YB)]
            for direction, block in pieces:
                d_pass(direction, block, i)
            for direction, block in pieces:
                d_finish(-i if direction == 0 else i, block)

    if outer:
        loads["o"].wait()
        loads["r"].wait()
    pl.semaphore_wait(barrier, expected)
    if outer:
        y_first()
    loads["x"].wait()
    loads["w"].wait()
    if inner:
        xt[...] = xv[...].reshape(toks, feats).T
        rows = rows_of(1 - c)
        for start, width in tiles:
            qoth[:, :, :, start:start + width] = partial(rows, start, width).astype(BF16)
        for k in (4, 3, 5, 2, 6, 1, 7, 0):
            net.start(("core", k), qoth.at[at_x(k)], qpar.at[at_x(k)], core)
    y_round(3)
    if inner:
        rows = rows_of(c)
        for start, width in tiles:
            qown[:, :, :, start:start + width] = partial(rows, start, width)
        for direction, block in x_order:
            x_send(direction, block, hops(direction, block, 2))
    y_round(2)
    x_round(3)
    y_round(1)
    x_round(2)
    if outer:
        for block in (0, 2, 1, 3):
            y_final(block)
    x_round(1)
    if inner:
        zs[...] = x_final(0).astype(BF16)
        net.start("zr", zs, zr, zlo)
        mine = x_final(1)
        loads["t"].wait()
        net.arrived("zr")
        total = mine + zr[...].astype(F32)
        ek[x, z, c, :, 0:cols] = (total[:, 0:cols] * weight_scale - tv[...].astype(F32)).astype(BF16)
        ek[x, z, c, :, cols:wide] = total[:, cols:wide].astype(BF16)
        slot = g_slot(0, 0)
        net.start("gz", slot, slot, zlo)
        g_own(0)
    g_hop(0, 1)
    if inner:
        net.arrived("gz")
        g_own(1)
    g_hop(0, 2)
    g_hop(1, 1)
    g_hop(0, 3)
    g_hop(1, 2)
    g_hop(0, 4)
    g_hop(1, 3)
    if outer:
        for block in (0, 2, 1, 3):
            d_own(block)
    g_hop(1, 4)
    if outer:
        loads["m"].wait()
        for block in range(YB):
            d_finish(0, block)
    d_hop(1)
    if inner:
        for name in list(net.made):
            if name[0] == "gc":
                net.arrived(name)
        turned = jnp.dot(xt[...], ek[:, :, :, :, cols:wide].reshape(toks, toks), preferred_element_type=F32)
        both = (2.0 * xt[...].astype(F32) - (inner_rate / D) * turned).astype(BF16)
    d_hop(2)
    if inner:
        for start in range(0, cols, cols // 2):
            at = slice(start, start + cols // 2)
            gradient = jnp.dot(both, ek[:, :, :, :, at].reshape(toks, cols // 2), preferred_element_type=F32)
            w_out[:, at] = wv[:, at] - (inner_rate * weight_scale) * gradient
    d_hop(3)
    d_hop(4)
    if not inner:
        loads["t"].wait()
    if not outer:
        loads["o"].wait()
        loads["r"].wait()
        loads["m"].wait()
    net.drain()


def exchange(tokens, targets, weights, outer_weights, moment, replica, inner=True, outer=True):
    toks, feats = tokens.shape
    cols = weights.shape[1]
    wide = cols + toks
    o_cols = outer_weights.shape[1]
    y_rows = outer_weights.shape[0] // NY
    weight_scale = D ** (-0.5)
    hbm = pl.BlockSpec(memory_space=pl.ANY)
    copies = 140
    results = pl.pallas_call(
        functools.partial(comm_kernel, inner, outer, weight_scale),
        out_shape=(
            jax.ShapeDtypeStruct((feats, cols), F32),
            jax.ShapeDtypeStruct((NY, y_rows, o_cols), F32),
            jax.ShapeDtypeStruct((NY, y_rows, o_cols), F32),
            jax.ShapeDtypeStruct((NY, y_rows, o_cols), BF16),
        ),
        in_specs=[hbm] * 6,
        out_specs=(pl.BlockSpec(memory_space=pltpu.VMEM),) * 4,
        scratch_shapes=[
            pltpu.VMEM((NX, NZ, NC, 16, feats), BF16),
            pltpu.VMEM((feats, toks), BF16),
            pltpu.VMEM((feats, cols), F32),
            pltpu.VMEM((16, cols), BF16),
            pltpu.VMEM((NY, y_rows, o_cols), F32),
            pltpu.VMEM((NY, y_rows, o_cols), BF16),
            pltpu.VMEM((NY, y_rows, o_cols), F32),
            pltpu.VMEM((NX, NZ, 16, wide), F32),
            pltpu.VMEM((NX, NZ, 16, wide), BF16),
            pltpu.VMEM((NX, NZ, 16, wide), BF16),
            pltpu.VMEM((2, 2, 4, 16, wide), BF16),
            pltpu.VMEM((2, 2, 4, 16, wide), BF16),
            pltpu.VMEM((16, wide), BF16),
            pltpu.VMEM((16, wide), BF16),
            pltpu.VMEM((NX, NZ, NC, 16, wide), BF16),
            pltpu.VMEM((2, YB, 4, y_rows, o_cols // YB), BF16),
            pltpu.VMEM((2, YB, 4, y_rows, o_cols // YB), BF16),
            pltpu.VMEM((y_rows, o_cols), F32),
            pltpu.VMEM((y_rows, o_cols), BF16),
            pltpu.VMEM((y_rows, o_cols), BF16),
            pltpu.VMEM((NY, y_rows, o_cols), BF16),
            pltpu.SemaphoreType.DMA((6,)),
            pltpu.SemaphoreType.DMA((copies,)),
            pltpu.SemaphoreType.DMA((copies,)),
        ],
        compiler_params=pltpu.CompilerParams(collective_id=0, has_side_effects=True, vmem_limit_bytes=32 << 20),
    )(
        *(pltpu.with_memory_space_constraint(array, pltpu.HBM) for array in (
            tokens.reshape(NX, NZ, NC, 16, feats),
            weights,
            targets,
            outer_weights.reshape(NY, y_rows, o_cols),
            replica.reshape(NY, y_rows, o_cols),
            moment.reshape(NY, y_rows, o_cols),
        ))
    )
    return results[0], *(result.reshape(outer_weights.shape) for result in results[1:])


def local(tokens, targets, inner_weights, outer_weights, outer_momentum, replica_weights):
    new_inner, new_outer, new_moment, merged = exchange(
        tokens[0], targets[0], inner_weights[0], outer_weights, outer_momentum, replica_weights[0]
    )
    return (new_inner[None], new_outer, new_moment, merged[None])


def solution(mesh):
    placed = (
        P("rep", None, "fsdp"),
        P("rep", "fsdp", None),
        P("rep", "fsdp", None),
        P("fsdp", None),
        P("fsdp", None),
        P("rep", "fsdp", None),
    )
    return jax.shard_map(
        local,
        mesh=mesh,
        in_specs=placed,
        out_specs=(
            P("rep", "fsdp", None),
            P("fsdp", None),
            P("fsdp", None),
            P("rep", "fsdp", None),
        ),
        check_vma=False,
    )
```

time: 74.2 us -> 72.3 us (0.974)
  local copies, waits for them, and re-layouts: 0.02 us -> 3.7 us
  other arithmetic: 3.51 us -> 0 us
  matrix products: 3.41 us -> 0 us
  Pallas kernels: 66.4 us -> 67.8 us
    unnamed x8 -> x4, local copies, waits for them, and re-layouts: 0.02 us -> 3.7 us
    broadcast_in_dim x1 -> x0, other arithmetic: 3.51 us -> none  [local(): return (new_inner[None], new_outer, new_moment, mixed.astype(BF16)[None])]
    dot_general x1 -> x0, matrix products: 3.41 us -> none  [local(): lax.dot_general(both, errors, (((0,), (0,)), ((), ())), preferred_element...]
    pallas_call x1, Pallas kernels: 66.4 us -> 67.8 us  [exchange(): pl.pallas_call(functools.partial(comm_kernel, inner, outer, weight_scale)...]
where the time goes in v2:
time: 72.3 us; the launch traced here: 72.2 us
  Pallas kernels  67.8 us (94%)
  local copies, waits for them, and re-layouts  3.7 us (5%)
    pallas_call x1, Pallas kernels, exchange(): pl.pallas_call(functools.partial(comm_kernel, inner, outer, weight_scale)...  67.8 us
    unnamed x4, local copies, waits for them, and re-layouts  3.7 us

profile of v2, /device:TPU:2, one launch (start us, length us, event | category | flops | bytes accessed | tf_op | source)
XLA Modules:
  0.0 72.2 jit_solution(673493750310887631)
XLA Ops:
  0.6 67.8 %shard_map.93 = (f32[256,1024]{1,0:T(8,128)S(1)}, f32[8,32,1024]{2,1,0:T(8,128)S(1)}, f32[8,32,1024]{2,1,0:T(8,128)S(1)}, bf16[8,32,1024]{2,1,0:T(8,128)(2,1)S(1)}) custom-call(bf16[8,2,2,16,256]{4,3,2,1,0:T(8,128)(2,1)} %bitcast.18, f32[256,1024]{1,0:T(8,128)} %bitcast.14, bf16[16,1024]{1,0:T(8,128)(2,1)} %bitcast.19, f32[8,32,1024]{2,1,0:T(8,128)} %bitcast.15, ...), custom_call_target="tpu_custom_call" | custom-call | tf_op jit(solution)/shard_map/pallas_call | solution.py:394
  68.5 1.0 %copy.14 = f32[1,256,1024]{2,1,0:T(8,128)} copy(f32[1,256,1024]{2,1,0:T(8,128)S(1)} %bitcast.12) | data formatting | bytes 2097152
  69.4 1.0 %copy.15 = f32[256,1024]{1,0:T(8,128)} copy(f32[256,1024]{1,0:T(8,128)S(1)} %bitcast.11) | data formatting | bytes 2097152
  70.4 1.0 %copy.16 = f32[256,1024]{1,0:T(8,128)} copy(f32[256,1024]{1,0:T(8,128)S(1)} %bitcast.10) | data formatting | bytes 2097152
  71.4 0.8 %copy.17 = bf16[1,256,1024]{2,1,0:T(8,128)(2,1)} copy(bf16[1,256,1024]{2,1,0:T(8,128)(2,1)S(1)} %bitcast.13) | data formatting | bytes 1048576

commit v3 on v2

--- a/solution.py
+++ b/solution.py
@@ -21,24 +21,26 @@
 
 
 class Copies:
-    def __init__(self, send_sems, recv_sems):
+    def __init__(self, send_sems, recv_sems, slots=None, made=None):
         self.send_sems, self.recv_sems = send_sems, recv_sems
-        self.made, self.guards, self.slots = {}, {}, 0
+        self.slots = {} if slots is None else slots
+        self.made = {} if made is None else dict(made)
+
+    def branch(self):
+        return Copies(self.send_sems, self.recv_sems, self.slots, self.made)
 
     def make(self, name, src, dst, device, recv_like=None, guard=None):
-        slot = self.slots
-        self.slots += 1
+        slot = self.slots.setdefault(name, len(self.slots))
         assert slot < self.send_sems.shape[0]
-        recv_slot = slot if recv_like is None else self.made[recv_like][1]
         copy = pltpu.make_async_remote_copy(
             src_ref=src,
             dst_ref=dst,
             send_sem=self.send_sems.at[slot],
-            recv_sem=self.recv_sems.at[recv_slot],
+            recv_sem=self.recv_sems.at[slot if recv_like is None else self.slots[recv_like]],
             device_id=device,
             device_id_type=MESH,
         )
-        self.made[name] = (copy, recv_slot, guard)
+        self.made[name] = (copy, guard)
         return copy
 
     def start(self, name, src, dst, device):
@@ -51,7 +53,7 @@
         self.made[name][0].wait_recv()
 
     def drain(self):
-        for copy, _, guard in self.made.values():
+        for copy, guard in self.made.values():
             if guard is None:
                 copy.wait_send()
             else:
@@ -69,6 +71,8 @@
 
 
 YB = 4
+XH = 2
+XB = 2 * XH
 
 
 def hops(direction, block, blocks):
@@ -77,7 +81,7 @@
 
 def comm_kernel(inner, outer, weight_scale, x_hbm, w_hbm, t_hbm, o_hbm, r_hbm, m_hbm,
                 w_out, o_out, m_out, r_out,
-                xv, xt, wv, tv, ov, rv, mv, qown, qoth, qpar, rx, sx, zs, zr, ek,
+                xv, xt, wv, wb, tv, ov, rv, mv, qown, qoth, qpar, rx, sx, zs, zr, ek,
                 ry, sy, ysum, us, ub, dv,
                 load_sems, send_sems, recv_sems):
     rep, fsdp = lax.axis_index("rep"), lax.axis_index("fsdp")
@@ -192,17 +196,15 @@
             for target in range(NH - 1):
                 net.begin(("down", block, target))
 
-    def rows_of(core_index):
-        return xv[:, :, core_index].reshape(NX * NZ * 16, feats)
-
-    def partial(rows, start, width):
-        if start < cols:
-            right = wv[:, start:start + width].astype(BF16)
-        else:
-            right = xt[...]
-        return jnp.dot(rows, right, preferred_element_type=F32).reshape(NX, NZ, 16, width)
-
     tiles = [(start, cols // 2) for start in (0, cols // 2)] + [(cols, toks)]
+
+    def partial(core_index, ks, out, dtype):
+        rows = jnp.concatenate([xv[at_x(k), :, core_index].reshape(NZ * 16, feats) for k in ks], axis=0)
+        for start, width in tiles:
+            right = wb[:, start:start + width] if start < cols else xt[...]
+            value = jnp.dot(rows, right, preferred_element_type=F32).astype(dtype)
+            for n, k in enumerate(ks):
+                out[at_x(k), :, :, start:start + width] = value[n * NZ * 16:(n + 1) * NZ * 16].reshape(NZ, 16, width)
 
     merged = set()
 
@@ -213,90 +215,192 @@
             net.arrived(("core", k))
             qown[at_x(k)] = qown[at_x(k)] + qpar[at_x(k)].astype(F32)
 
+    xcols = wide // XH
+
+    def xcut(block):
+        return slice((block % XH) * xcols, (block % XH + 1) * xcols)
+
     def zz(block):
-        return 1 - z if block == 0 else z
+        return 1 - z if block < XH else z
 
     def x_send(direction, block, j):
         step = 1 if direction == 0 else -1
         merge(step * j)
-        value = qown[at_x(step * j), zz(block)]
-        if j < hops(direction, block, 2):
+        value = qown[at_x(step * j), zz(block), :, xcut(block)]
+        if j < hops(direction, block, XB):
             net.arrived(("rx", direction, block, j + 1))
             value = value + rx[direction, block, j].astype(F32)
         sx[direction, block, j - 1] = value.astype(BF16)
         net.start(("rx", direction, block, j), sx.at[direction, block, j - 1], rx.at[direction, block, j - 1], to_x(step))
 
-    def x_final(block):
-        merge(0)
+    def x_final(net, block):
         for direction in (0, 1):
             net.arrived(("rx", direction, block, 1))
-        return qown[x, zz(block)] + (rx[0, block, 0].astype(F32) + rx[1, block, 0].astype(F32))
-
-    x_order = ((0, 0), (1, 1), (0, 1), (1, 0))
+        return qown[x, zz(block), :, xcut(block)] + (rx[0, block, 0].astype(F32) + rx[1, block, 0].astype(F32))
+
+    def halves(first_block, other_block):
+        return [((0, first_block + n), (1, other_block + n)) for n in range(XH)]
+
+    x_long = [pair for pairs in halves(0, XH) for pair in pairs]
+    x_short = [pair for pairs in halves(XH, 0) for pair in pairs]
+    x_order = x_long + x_short
 
     def x_round(j):
         if inner:
             for direction, block in x_order:
-                if j < hops(direction, block, 2):
+                if j < hops(direction, block, XB):
                     x_send(direction, block, j)
 
     def g_slot(k, block):
-        return ek.at[at_x(k), z if block == 0 else 1 - z, c]
-
-    def g_pass(direction, block, i):
-        step = 1 if direction == 0 else -1
-        slot = g_slot(-step * i, block)
-        if i > 0:
-            net.arrived(("gx", direction, block, i))
-        if i < hops(direction, block, 2):
-            net.start(("gx", direction, block, i + 1), slot, slot, to_x(step))
-        if i > 0:
-            net.start(("gc", direction, block, i), slot, slot, core)
-
-    def g_own(block):
-        slot = g_slot(0, block)
-        for direction in (0, 1):
-            g_pass(direction, block, 0)
-        net.start(("gc", block), slot, slot, core)
-
-    def g_hop(block, i):
-        if inner:
+        return ek.at[at_x(k), z if block < XH else 1 - z, c, :, xcut(block)]
+
+    def rest(net, late):
+        def g_pass(direction, block, i):
+            step = 1 if direction == 0 else -1
+            slot = g_slot(-step * i, block)
+            if i > 0:
+                net.arrived(("gx", direction, block, i))
+            if i < hops(direction, block, XB):
+                net.start(("gx", direction, block, i + 1), slot, slot, to_x(step))
+            if i > 0:
+                net.start(("gc", direction, block, i), slot, slot, core)
+
+        def g_own(block):
             for direction in (0, 1):
-                if i <= hops(direction, block, 2):
-                    g_pass(direction, block, i)
-
-    def d_pass(direction, block, i):
-        step = 1 if direction == 0 else -1
-        slot = dv.at[at_y(-step * i), :, ycut(block)]
-        if i > 0:
-            net.arrived(("gy", direction, block, i))
-        if i < hops(direction, block, YB):
-            net.start(("gy", direction, block, i + 1), slot, slot, to_y(step))
-
-    def d_own(block):
-        @pl.when(jnp.logical_not(last))
-        def _():
-            net.arrived(("down", block, 0))
-
-        for direction in (0, 1):
-            d_pass(direction, block, 0)
-
-    def d_finish(k, block):
-        at, row = ycut(block), at_y(k)
-        delta = dec(dv[row, :, at])
-        moment = momentum_coef * mv[row, :, at] + delta
-        moved = ov[row, :, at] - outer_rate * (delta + momentum_coef * moment)
-        m_out[row, :, at] = moment
-        o_out[row, :, at] = moved
-        r_out[row, :, at] = (merge_keep * rv[row, :, at].astype(F32) + (1.0 - merge_keep) * moved).astype(BF16)
-
-    def d_hop(i):
-        if outer:
-            pieces = [piece for piece in y_order if i <= hops(*piece, YB)]
-            for direction, block in pieces:
-                d_pass(direction, block, i)
-            for direction, block in pieces:
-                d_finish(-i if direction == 0 else i, block)
+                g_pass(direction, block, 0)
+            net.start(("gc", block), g_slot(0, block), g_slot(0, block), core)
+
+        def g_hop(side, i):
+            if inner:
+                for block in range(side * XH, (side + 1) * XH):
+                    for direction in (0, 1):
+                        if i <= hops(direction, block, XB):
+                            g_pass(direction, block, i)
+
+        def d_pass(direction, block, i):
+            step = 1 if direction == 0 else -1
+            slot = dv.at[at_y(-step * i), :, ycut(block)]
+            if i > 0:
+                net.arrived(("gy", direction, block, i))
+            if i < hops(direction, block, YB):
+                net.start(("gy", direction, block, i + 1), slot, slot, to_y(step))
+
+        def d_finish(k, block):
+            at, row = ycut(block), at_y(k)
+            delta = dec(dv[row, :, at])
+            moment = momentum_coef * mv[row, :, at] + delta
+            moved = ov[row, :, at] - outer_rate * (delta + momentum_coef * moment)
+            m_out[row, :, at] = moment
+            o_out[row, :, at] = moved
+            r_out[row, :, at] = (merge_keep * rv[row, :, at].astype(F32) + (1.0 - merge_keep) * moved).astype(BF16)
+
+        def d_own():
+            if outer:
+                for block in (0, 2, 1, 3):
+                    @pl.when(jnp.logical_not(last))
+                    def _():
+                        net.arrived(("down", block, 0))
+
+                    for direction in (0, 1):
+                        d_pass(direction, block, 0)
+
+        def d_own_finish():
+            loads["m"].wait()
+            if outer:
+                for block in range(YB):
+                    d_finish(0, block)
+
+        def d_hop(i):
+            if outer:
+                pieces = [piece for piece in y_order if i <= hops(*piece, YB)]
+                for direction, block in pieces:
+                    d_pass(direction, block, i)
+                for direction, block in pieces:
+                    d_finish(-i if direction == 0 else i, block)
+
+        def z_sends():
+            if inner:
+                for n in range(XH):
+                    zs[:, xcut(n)] = x_final(net, n).astype(BF16)
+                    net.start(("zr", n), zs.at[:, xcut(n)], zr.at[:, xcut(n)], zlo)
+
+        def own_errors():
+            if inner:
+                loads["t"].wait()
+                for n in range(XH):
+                    mine = x_final(net, XH + n)
+                    net.arrived(("zr", n))
+                    total = mine + zr[:, xcut(n)].astype(F32)
+                    low, high = n * xcols, (n + 1) * xcols
+                    edge = min(max(cols, low), high)
+                    if low < edge:
+                        ek[x, z, c, :, low:edge] = (total[:, :edge - low] * weight_scale - tv[:, low:edge].astype(F32)).astype(BF16)
+                    if edge < high:
+                        ek[x, z, c, :, edge:high] = total[:, edge - low:].astype(BF16)
+                    net.start(("gz", n), g_slot(0, n), g_slot(0, n), zlo)
+                    g_own(n)
+
+        def neighbour_errors():
+            if inner:
+                for n in range(XH):
+                    net.arrived(("gz", n))
+                    g_own(XH + n)
+
+        def core_errors():
+            if inner:
+                for name in list(net.made):
+                    if name[0] == "gc":
+                        net.arrived(name)
+
+        def last_product():
+            if inner:
+                turned = jnp.dot(xt[...], ek[:, :, :, :, cols:wide].reshape(toks, toks), preferred_element_type=F32)
+                both = (2.0 * xt[...].astype(F32) - (inner_rate / D) * turned).astype(BF16)
+                for start in range(0, cols, cols // 2):
+                    at = slice(start, start + cols // 2)
+                    gradient = jnp.dot(both, ek[:, :, :, :, at].reshape(toks, cols // 2), preferred_element_type=F32)
+                    w_out[:, at] = wv[:, at] - (inner_rate * weight_scale) * gradient
+
+        z_sends()
+        if late:
+            d_own()
+            own_errors()
+            d_own_finish()
+            d_hop(1)
+            g_hop(0, 1)
+            neighbour_errors()
+            d_hop(2)
+            g_hop(0, 2)
+            g_hop(1, 1)
+            d_hop(3)
+            g_hop(0, 3)
+            g_hop(1, 2)
+            d_hop(4)
+            g_hop(0, 4)
+            g_hop(1, 3)
+            g_hop(1, 4)
+            core_errors()
+            last_product()
+        else:
+            own_errors()
+            g_hop(0, 1)
+            neighbour_errors()
+            g_hop(0, 2)
+            g_hop(1, 1)
+            g_hop(0, 3)
+            g_hop(1, 2)
+            d_own()
+            g_hop(0, 4)
+            g_hop(1, 3)
+            d_own_finish()
+            d_hop(1)
+            g_hop(1, 4)
+            d_hop(2)
+            core_errors()
+            last_product()
+            d_hop(3)
+            d_hop(4)
+        net.drain()
 
     if outer:
         loads["o"].wait()
@@ -305,21 +409,20 @@
     if outer:
         y_first()
     loads["x"].wait()
+    if inner:
+        xt[...] = xv[...].reshape(toks, feats).T
     loads["w"].wait()
     if inner:
-        xt[...] = xv[...].reshape(toks, feats).T
-        rows = rows_of(1 - c)
-        for start, width in tiles:
-            qoth[:, :, :, start:start + width] = partial(rows, start, width).astype(BF16)
-        for k in (4, 3, 5, 2, 6, 1, 7, 0):
-            net.start(("core", k), qoth.at[at_x(k)], qpar.at[at_x(k)], core)
+        wb[...] = wv[...].astype(BF16)
+        for ks in ((4, 3), (5, 2), (6, 1), (7, 0)):
+            partial(1 - c, ks, qoth, BF16)
+            for k in ks:
+                net.start(("core", k), qoth.at[at_x(k)], qpar.at[at_x(k)], core)
     y_round(3)
     if inner:
-        rows = rows_of(c)
-        for start, width in tiles:
-            qown[:, :, :, start:start + width] = partial(rows, start, width)
+        partial(c, (4, 3, 5, 2, 6, 1, 7, 0), qown, F32)
         for direction, block in x_order:
-            x_send(direction, block, hops(direction, block, 2))
+            x_send(direction, block, hops(direction, block, XB))
     y_round(2)
     x_round(3)
     y_round(1)
@@ -329,57 +432,41 @@
             y_final(block)
     x_round(1)
     if inner:
-        zs[...] = x_final(0).astype(BF16)
-        net.start("zr", zs, zr, zlo)
-        mine = x_final(1)
-        loads["t"].wait()
-        net.arrived("zr")
-        total = mine + zr[...].astype(F32)
-        ek[x, z, c, :, 0:cols] = (total[:, 0:cols] * weight_scale - tv[...].astype(F32)).astype(BF16)
-        ek[x, z, c, :, cols:wide] = total[:, cols:wide].astype(BF16)
-        slot = g_slot(0, 0)
-        net.start("gz", slot, slot, zlo)
-        g_own(0)
-    g_hop(0, 1)
-    if inner:
-        net.arrived("gz")
-        g_own(1)
-    g_hop(0, 2)
-    g_hop(1, 1)
-    g_hop(0, 3)
-    g_hop(1, 2)
-    g_hop(0, 4)
-    g_hop(1, 3)
-    if outer:
-        for block in (0, 2, 1, 3):
-            d_own(block)
-    g_hop(1, 4)
-    if outer:
-        loads["m"].wait()
-        for block in range(YB):
-            d_finish(0, block)
-    d_hop(1)
-    if inner:
-        for name in list(net.made):
-            if name[0] == "gc":
-                net.arrived(name)
-        turned = jnp.dot(xt[...], ek[:, :, :, :, cols:wide].reshape(toks, toks), preferred_element_type=F32)
-        both = (2.0 * xt[...].astype(F32) - (inner_rate / D) * turned).astype(BF16)
-    d_hop(2)
-    if inner:
-        for start in range(0, cols, cols // 2):
-            at = slice(start, start + cols // 2)
-            gradient = jnp.dot(both, ek[:, :, :, :, at].reshape(toks, cols // 2), preferred_element_type=F32)
-            w_out[:, at] = wv[:, at] - (inner_rate * weight_scale) * gradient
-    d_hop(3)
-    d_hop(4)
+        merge(0)
     if not inner:
         loads["t"].wait()
     if not outer:
         loads["o"].wait()
         loads["r"].wait()
-        loads["m"].wait()
-    net.drain()
+
+    @pl.when(h >= NH // 2)
+    def _():
+        rest(net.branch(), True)
+
+    @pl.when(h < NH // 2)
+    def _():
+        rest(net.branch(), False)
+
+
+def store_kernel(*refs):
+    sems = refs[-1]
+    half = (len(refs) - 1) // 2
+    stores = [pltpu.make_async_copy(refs[n], refs[half + n], sems.at[n]) for n in range(half)]
+    for store in stores:
+        store.start()
+    for store in stores:
+        store.wait()
+
+
+def store_results(results):
+    return pl.pallas_call(
+        store_kernel,
+        out_shape=tuple(pltpu.HBM(result.shape, result.dtype) for result in results),
+        in_specs=[pl.BlockSpec(memory_space=pl.ANY)] * len(results),
+        out_specs=(pl.BlockSpec(memory_space=pltpu.HBM),) * len(results),
+        scratch_shapes=[pltpu.SemaphoreType.DMA((len(results),))],
+        compiler_params=pltpu.CompilerParams(vmem_limit_bytes=2 << 20),
+    )(*results)
 
 
 def exchange(tokens, targets, weights, outer_weights, moment, replica, inner=True, outer=True):
@@ -390,7 +477,7 @@
     y_rows = outer_weights.shape[0] // NY
     weight_scale = D ** (-0.5)
     hbm = pl.BlockSpec(memory_space=pl.ANY)
-    copies = 140
+    copies = 200
     results = pl.pallas_call(
         functools.partial(comm_kernel, inner, outer, weight_scale),
         out_shape=(
@@ -405,6 +492,7 @@
             pltpu.VMEM((NX, NZ, NC, 16, feats), BF16),
             pltpu.VMEM((feats, toks), BF16),
             pltpu.VMEM((feats, cols), F32),
+            pltpu.VMEM((feats, cols), BF16),
             pltpu.VMEM((16, cols), BF16),
             pltpu.VMEM((NY, y_rows, o_cols), F32),
             pltpu.VMEM((NY, y_rows, o_cols), BF16),
@@ -412,8 +500,8 @@
             pltpu.VMEM((NX, NZ, 16, wide), F32),
             pltpu.VMEM((NX, NZ, 16, wide), BF16),
             pltpu.VMEM((NX, NZ, 16, wide), BF16),
-            pltpu.VMEM((2, 2, 4, 16, wide), BF16),
-            pltpu.VMEM((2, 2, 4, 16, wide), BF16),
+            pltpu.VMEM((2, XB, 4, 16, wide // XH), BF16),
+            pltpu.VMEM((2, XB, 4, 16, wide // XH), BF16),
             pltpu.VMEM((16, wide), BF16),
             pltpu.VMEM((16, wide), BF16),
             pltpu.VMEM((NX, NZ, NC, 16, wide), BF16),
@@ -442,9 +530,9 @@
 
 
 def local(tokens, targets, inner_weights, outer_weights, outer_momentum, replica_weights):
-    new_inner, new_outer, new_moment, merged = exchange(
+    new_inner, new_outer, new_moment, merged = store_results(exchange(
         tokens[0], targets[0], inner_weights[0], outer_weights, outer_momentum, replica_weights[0]
-    )
+    ))
     return (new_inner[None], new_outer, new_moment, merged[None])
 
 

time: 72.3 us -> 66.4 us (0.918)
  the two profiles are of different devices: /device:TPU:2 before, /device:TPU:258 now
where the time goes in v3:
time: 66.4 us; the launch traced here: 66.3 us
  Pallas kernels  65.6 us (99%)
    pallas_call x1, Pallas kernels, exchange(): pl.pallas_call(functools.partial(comm_kernel, inner, outer, weight_scale)...  63.8 us
    pallas_call x1, Pallas kernels, store_results(): pl.pallas_call(store_kernel, out_shape=tuple((pltpu.HBM(result.shape, res...  1.87 us

profile of v3, /device:TPU:258, one launch (start us, length us, event | category | flops | bytes accessed | tf_op | source)
XLA Modules:
  0.0 66.3 jit_solution(8762162521052665906)
XLA Ops:
  0.6 63.8 %shard_map.93 = (f32[256,1024]{1,0:T(8,128)S(1)}, f32[8,32,1024]{2,1,0:T(8,128)S(1)}, f32[8,32,1024]{2,1,0:T(8,128)S(1)}, bf16[8,32,1024]{2,1,0:T(8,128)(2,1)S(1)}) custom-call(bf16[8,2,2,16,256]{4,3,2,1,0:T(8,128)(2,1)} %bitcast.18, f32[256,1024]{1,0:T(8,128)} %bitcast.14, bf16[16,1024]{1,0:T(8,128)(2,1)} %bitcast.19, f32[8,32,1024]{2,1,0:T(8,128)} %bitcast.15, ...), custom_call_target="tpu_custom_call" | custom-call | tf_op jit(solution)/shard_map/pallas_call | solution.py:481
  64.4 1.9 %shard_map.94 = (f32[256,1024]{1,0:T(8,128)}, f32[256,1024]{1,0:T(8,128)}, f32[256,1024]{1,0:T(8,128)}, bf16[256,1024]{1,0:T(8,128)(2,1)}) custom-call(f32[256,1024]{1,0:T(8,128)S(1)} %get-tuple-element.12.refs_0_, f32[256,1024]{1,0:T(8,128)S(1)} %bitcast.11, f32[256,1024]{1,0:T(8,128)S(1)} %bitcast.12, bf16[256,1024]{1,0:T(8,128)(2,1)S(1)} %bitcast.13), custom_call_target="tpu_custom_call" | custom-call | tf_op jit(solution)/shard_map/pallas_call | solution.py:462

commit v4 on v3

--- a/solution.py
+++ b/solution.py
@@ -175,26 +175,32 @@
             net.arrived(("ry", direction, block, 1))
         at = ycut(block)
         ysum[:, at] = y_own(0, block) + (dec(ry[0, block, 0]) + dec(ry[1, block, 0]))
-        net.make(("up", block), us.at[:, at], ub.at[:, at], to_h(above), guard=jnp.logical_not(last))
-        slot = dv.at[y, :, at]
+        net.make(("up", block), us.at[block], ub.at[block], to_h(above), guard=jnp.logical_not(last))
+        slot = dv.at[y, block]
         for target in range(NH - 1):
             net.make(("down", block, target), slot, slot, to_h(target), recv_like=("down", block, 0) if target else None, guard=last)
 
         @pl.when(jnp.logical_not(first))
         def _():
             net.arrived(("up", block))
-            ysum[:, at] = ysum[:, at] + dec(ub[:, at])
+            ysum[:, at] = ysum[:, at] + dec(ub[block])
 
         @pl.when(jnp.logical_not(last))
         def _():
-            us[:, at] = enc(ysum[:, at])
+            us[block] = enc(ysum[:, at])
             net.begin(("up", block))
 
         @pl.when(last)
         def _():
-            dv[y, :, at] = enc(ysum[:, at] / REPS)
-            for target in range(NH - 1):
-                net.begin(("down", block, target))
+            dv[y, block] = enc(ysum[:, at] / REPS)
+            net.begin(("down", block, 0))
+
+    def y_spread():
+        @pl.when(last)
+        def _():
+            for target in range(1, NH - 1):
+                for block in range(YB):
+                    net.begin(("down", block, target))
 
     tiles = [(start, cols // 2) for start in (0, cols // 2)] + [(cols, toks)]
 
@@ -279,7 +285,7 @@
 
         def d_pass(direction, block, i):
             step = 1 if direction == 0 else -1
-            slot = dv.at[at_y(-step * i), :, ycut(block)]
+            slot = dv.at[at_y(-step * i), block]
             if i > 0:
                 net.arrived(("gy", direction, block, i))
             if i < hops(direction, block, YB):
@@ -287,7 +293,7 @@
 
         def d_finish(k, block):
             at, row = ycut(block), at_y(k)
-            delta = dec(dv[row, :, at])
+            delta = dec(dv[row, block])
             moment = momentum_coef * mv[row, :, at] + delta
             moved = ov[row, :, at] - outer_rate * (delta + momentum_coef * moment)
             m_out[row, :, at] = moment
@@ -390,15 +396,15 @@
             g_hop(0, 3)
             g_hop(1, 2)
             d_own()
+            d_own_finish()
+            d_hop(1)
             g_hop(0, 4)
             g_hop(1, 3)
-            d_own_finish()
-            d_hop(1)
+            d_hop(2)
             g_hop(1, 4)
-            d_hop(2)
+            d_hop(3)
             core_errors()
             last_product()
-            d_hop(3)
             d_hop(4)
         net.drain()
 
@@ -421,15 +427,17 @@
     y_round(3)
     if inner:
         partial(c, (4, 3, 5, 2, 6, 1, 7, 0), qown, F32)
+    y_round(2)
+    if inner:
         for direction, block in x_order:
             x_send(direction, block, hops(direction, block, XB))
-    y_round(2)
+    y_round(1)
     x_round(3)
-    y_round(1)
-    x_round(2)
     if outer:
         for block in (0, 2, 1, 3):
             y_final(block)
+        y_spread()
+    x_round(2)
     x_round(1)
     if inner:
         merge(0)
@@ -508,9 +516,9 @@
             pltpu.VMEM((2, YB, 4, y_rows, o_cols // YB), BF16),
             pltpu.VMEM((2, YB, 4, y_rows, o_cols // YB), BF16),
             pltpu.VMEM((y_rows, o_cols), F32),
-            pltpu.VMEM((y_rows, o_cols), BF16),
-            pltpu.VMEM((y_rows, o_cols), BF16),
-            pltpu.VMEM((NY, y_rows, o_cols), BF16),
+            pltpu.VMEM((YB, y_rows, o_cols // YB), BF16),
+            pltpu.VMEM((YB, y_rows, o_cols // YB), BF16),
+            pltpu.VMEM((NY, YB, y_rows, o_cols // YB), BF16),
             pltpu.SemaphoreType.DMA((6,)),
             pltpu.SemaphoreType.DMA((copies,)),
             pltpu.SemaphoreType.DMA((copies,)),

time: 66.4 us -> 68.5 us (1.032)
  the two profiles are of different devices: /device:TPU:258 before, /device:TPU:256 now
where the time goes in v4:
time: 68.5 us; the launch traced here: 68.4 us
  Pallas kernels  67.7 us (99%)
    pallas_call x1, Pallas kernels, exchange(): pl.pallas_call(functools.partial(comm_kernel, inner, outer, weight_scale)...  65.9 us
    pallas_call x1, Pallas kernels, store_results(): pl.pallas_call(store_kernel, out_shape=tuple((pltpu.HBM(result.shape, res...  1.87 us

profile of v4, /device:TPU:256, one launch (start us, length us, event | category | flops | bytes accessed | tf_op | source)
XLA Modules:
  0.0 68.4 jit_solution(10058692385824673864)
XLA Ops:
  0.6 65.9 %shard_map.93 = (f32[256,1024]{1,0:T(8,128)S(1)}, f32[8,32,1024]{2,1,0:T(8,128)S(1)}, f32[8,32,1024]{2,1,0:T(8,128)S(1)}, bf16[8,32,1024]{2,1,0:T(8,128)(2,1)S(1)}) custom-call(bf16[8,2,2,16,256]{4,3,2,1,0:T(8,128)(2,1)} %bitcast.18, f32[256,1024]{1,0:T(8,128)} %bitcast.14, bf16[16,1024]{1,0:T(8,128)(2,1)} %bitcast.19, f32[8,32,1024]{2,1,0:T(8,128)} %bitcast.15, ...), custom_call_target="tpu_custom_call" | custom-call | tf_op jit(solution)/shard_map/pallas_call | solution.py:489
  66.5 1.9 %shard_map.94 = (f32[256,1024]{1,0:T(8,128)}, f32[256,1024]{1,0:T(8,128)}, f32[256,1024]{1,0:T(8,128)}, bf16[256,1024]{1,0:T(8,128)(2,1)}) custom-call(f32[256,1024]{1,0:T(8,128)S(1)} %get-tuple-element.12.refs_0_, f32[256,1024]{1,0:T(8,128)S(1)} %bitcast.11, f32[256,1024]{1,0:T(8,128)S(1)} %bitcast.12, bf16[256,1024]{1,0:T(8,128)(2,1)S(1)} %bitcast.13), custom_call_target="tpu_custom_call" | custom-call | tf_op jit(solution)/shard_map/pallas_call | solution.py:470

commit v5 on v4

--- a/solution.py
+++ b/solution.py
@@ -149,7 +149,7 @@
     def y_own(k, block):
         return ov[at_y(k), :, ycut(block)] - rv[at_y(k), :, ycut(block)].astype(F32)
 
-    def y_send(direction, block, j):
+    def y_send(net, direction, block, j):
         step = 1 if direction == 0 else -1
         value = y_own(step * j, block)
         if j < hops(direction, block, YB):
@@ -162,45 +162,7 @@
 
     def y_first():
         for direction, block in y_order:
-            y_send(direction, block, hops(direction, block, YB))
-
-    def y_round(j):
-        if outer:
-            for direction, block in y_order:
-                if j < hops(direction, block, YB):
-                    y_send(direction, block, j)
-
-    def y_final(block):
-        for direction in (0, 1):
-            net.arrived(("ry", direction, block, 1))
-        at = ycut(block)
-        ysum[:, at] = y_own(0, block) + (dec(ry[0, block, 0]) + dec(ry[1, block, 0]))
-        net.make(("up", block), us.at[block], ub.at[block], to_h(above), guard=jnp.logical_not(last))
-        slot = dv.at[y, block]
-        for target in range(NH - 1):
-            net.make(("down", block, target), slot, slot, to_h(target), recv_like=("down", block, 0) if target else None, guard=last)
-
-        @pl.when(jnp.logical_not(first))
-        def _():
-            net.arrived(("up", block))
-            ysum[:, at] = ysum[:, at] + dec(ub[block])
-
-        @pl.when(jnp.logical_not(last))
-        def _():
-            us[block] = enc(ysum[:, at])
-            net.begin(("up", block))
-
-        @pl.when(last)
-        def _():
-            dv[y, block] = enc(ysum[:, at] / REPS)
-            net.begin(("down", block, 0))
-
-    def y_spread():
-        @pl.when(last)
-        def _():
-            for target in range(1, NH - 1):
-                for block in range(YB):
-                    net.begin(("down", block, target))
+            y_send(net, direction, block, hops(direction, block, YB))
 
     tiles = [(start, cols // 2) for start in (0, cols // 2)] + [(cols, toks)]
 
@@ -212,55 +174,93 @@
             for n, k in enumerate(ks):
                 out[at_x(k), :, :, start:start + width] = value[n * NZ * 16:(n + 1) * NZ * 16].reshape(NZ, 16, width)
 
-    merged = set()
-
-    def merge(k):
-        k = k % NX
-        if k not in merged:
-            merged.add(k)
-            net.arrived(("core", k))
-            qown[at_x(k)] = qown[at_x(k)] + qpar[at_x(k)].astype(F32)
-
-    xcols = wide // XH
-
-    def xcut(block):
-        return slice((block % XH) * xcols, (block % XH + 1) * xcols)
-
-    def zz(block):
-        return 1 - z if block < XH else z
-
-    def x_send(direction, block, j):
-        step = 1 if direction == 0 else -1
-        merge(step * j)
-        value = qown[at_x(step * j), zz(block), :, xcut(block)]
-        if j < hops(direction, block, XB):
-            net.arrived(("rx", direction, block, j + 1))
-            value = value + rx[direction, block, j].astype(F32)
-        sx[direction, block, j - 1] = value.astype(BF16)
-        net.start(("rx", direction, block, j), sx.at[direction, block, j - 1], rx.at[direction, block, j - 1], to_x(step))
-
-    def x_final(net, block):
-        for direction in (0, 1):
-            net.arrived(("rx", direction, block, 1))
-        return qown[x, zz(block), :, xcut(block)] + (rx[0, block, 0].astype(F32) + rx[1, block, 0].astype(F32))
-
-    def halves(first_block, other_block):
-        return [((0, first_block + n), (1, other_block + n)) for n in range(XH)]
-
-    x_long = [pair for pairs in halves(0, XH) for pair in pairs]
-    x_short = [pair for pairs in halves(XH, 0) for pair in pairs]
-    x_order = x_long + x_short
-
-    def x_round(j):
-        if inner:
-            for direction, block in x_order:
-                if j < hops(direction, block, XB):
-                    x_send(direction, block, j)
-
-    def g_slot(k, block):
-        return ek.at[at_x(k), z if block < XH else 1 - z, c, :, xcut(block)]
-
     def rest(net, late):
+        merged = set()
+
+        def y_round(j):
+            if outer:
+                for direction, block in y_order:
+                    if j < hops(direction, block, YB):
+                        y_send(net, direction, block, j)
+
+        def y_final(block):
+            for direction in (0, 1):
+                net.arrived(("ry", direction, block, 1))
+            at = ycut(block)
+            ysum[:, at] = y_own(0, block) + (dec(ry[0, block, 0]) + dec(ry[1, block, 0]))
+            net.make(("up", block), us.at[block], ub.at[block], to_h(above), guard=jnp.logical_not(last))
+            slot = dv.at[y, block]
+            for target in range(NH - 1):
+                net.make(("down", block, target), slot, slot, to_h(target), recv_like=("down", block, 0) if target else None, guard=last)
+
+            @pl.when(jnp.logical_not(first))
+            def _():
+                net.arrived(("up", block))
+                ysum[:, at] = ysum[:, at] + dec(ub[block])
+
+            @pl.when(jnp.logical_not(last))
+            def _():
+                us[block] = enc(ysum[:, at])
+                net.begin(("up", block))
+
+            @pl.when(last)
+            def _():
+                dv[y, block] = enc(ysum[:, at] / REPS)
+                net.begin(("down", block, 0))
+
+        def y_spread():
+            @pl.when(last)
+            def _():
+                for target in range(1, NH - 1):
+                    for block in range(YB):
+                        net.begin(("down", block, target))
+
+        def merge(k):
+            k = k % NX
+            if k not in merged:
+                merged.add(k)
+                net.arrived(("core", k))
+                qown[at_x(k)] = qown[at_x(k)] + qpar[at_x(k)].astype(F32)
+
+        xcols = wide // XH
+
+        def xcut(block):
+            return slice((block % XH) * xcols, (block % XH + 1) * xcols)
+
+        def zz(block):
+            return 1 - z if block < XH else z
+
+        def x_send(direction, block, j):
+            step = 1 if direction == 0 else -1
+            merge(step * j)
+            value = qown[at_x(step * j), zz(block), :, xcut(block)]
+            if j < hops(direction, block, XB):
+                net.arrived(("rx", direction, block, j + 1))
+                value = value + rx[direction, block, j].astype(F32)
+            sx[direction, block, j - 1] = value.astype(BF16)
+            net.start(("rx", direction, block, j), sx.at[direction, block, j - 1], rx.at[direction, block, j - 1], to_x(step))
+
+        def x_final(net, block):
+            for direction in (0, 1):
+                net.arrived(("rx", direction, block, 1))
+            return qown[x, zz(block), :, xcut(block)] + (rx[0, block, 0].astype(F32) + rx[1, block, 0].astype(F32))
+
+        def halves(first_block, other_block):
+            return [((0, first_block + n), (1, other_block + n)) for n in range(XH)]
+
+        x_long = [pair for pairs in halves(0, XH) for pair in pairs]
+        x_short = [pair for pairs in halves(XH, 0) for pair in pairs]
+        x_order = x_long + x_short
+
+        def x_round(j):
+            if inner:
+                for direction, block in x_order:
+                    if j < hops(direction, block, XB):
+                        x_send(direction, block, j)
+
+        def g_slot(k, block):
+            return ek.at[at_x(k), z if block < XH else 1 - z, c, :, xcut(block)]
+
         def g_pass(direction, block, i):
             step = 1 if direction == 0 else -1
             slot = g_slot(-step * i, block)
@@ -367,7 +367,39 @@
                     gradient = jnp.dot(both, ek[:, :, :, :, at].reshape(toks, cols // 2), preferred_element_type=F32)
                     w_out[:, at] = wv[:, at] - (inner_rate * weight_scale) * gradient
 
+        def x_first():
+            if inner:
+                for direction, block in x_order:
+                    x_send(direction, block, hops(direction, block, XB))
+
+        def y_finals():
+            if outer:
+                for block in (0, 2, 1, 3):
+                    y_final(block)
+                y_spread()
+
+        if late:
+            y_round(3)
+            y_round(2)
+            x_first()
+            y_round(1)
+            x_round(3)
+            y_finals()
+            x_round(2)
+            x_round(1)
+        else:
+            x_first()
+            y_round(3)
+            x_round(3)
+            y_round(2)
+            x_round(2)
+            y_round(1)
+            x_round(1)
+        if inner:
+            merge(0)
         z_sends()
+        if not late:
+            y_finals()
         if late:
             d_own()
             own_errors()
@@ -424,23 +456,8 @@
             partial(1 - c, ks, qoth, BF16)
             for k in ks:
                 net.start(("core", k), qoth.at[at_x(k)], qpar.at[at_x(k)], core)
-    y_round(3)
     if inner:
         partial(c, (4, 3, 5, 2, 6, 1, 7, 0), qown, F32)
-    y_round(2)
-    if inner:
-        for direction, block in x_order:
-            x_send(direction, block, hops(direction, block, XB))
-    y_round(1)
-    x_round(3)
-    if outer:
-        for block in (0, 2, 1, 3):
-            y_final(block)
-        y_spread()
-    x_round(2)
-    x_round(1)
-    if inner:
-        merge(0)
     if not inner:
         loads["t"].wait()
     if not outer:

time: 68.5 us -> 66 us (0.964)
  the two profiles are of different devices: /device:TPU:256 before, /device:TPU:769 now
where the time goes in v5:
time: 66 us; the launch traced here: 65.9 us
  Pallas kernels  65.2 us (99%)
    pallas_call x1, Pallas kernels, exchange(): pl.pallas_call(functools.partial(comm_kernel, inner, outer, weight_scale)...  63.4 us
    pallas_call x1, Pallas kernels, store_results(): pl.pallas_call(store_kernel, out_shape=tuple((pltpu.HBM(result.shape, res...  1.87 us

profile of v5, /device:TPU:769, one launch (start us, length us, event | category | flops | bytes accessed | tf_op | source)
XLA Modules:
  0.0 65.9 jit_solution(3519474489657709732)
XLA Ops:
  0.6 63.4 %shard_map.93 = (f32[256,1024]{1,0:T(8,128)S(1)}, f32[8,32,1024]{2,1,0:T(8,128)S(1)}, f32[8,32,1024]{2,1,0:T(8,128)S(1)}, bf16[8,32,1024]{2,1,0:T(8,128)(2,1)S(1)}) custom-call(bf16[8,2,2,16,256]{4,3,2,1,0:T(8,128)(2,1)} %bitcast.18, f32[256,1024]{1,0:T(8,128)} %bitcast.14, bf16[16,1024]{1,0:T(8,128)(2,1)} %bitcast.19, f32[8,32,1024]{2,1,0:T(8,128)} %bitcast.15, ...), custom_call_target="tpu_custom_call" | custom-call | tf_op jit(solution)/shard_map/pallas_call | solution.py:506
  64.0 1.9 %shard_map.94 = (f32[256,1024]{1,0:T(8,128)}, f32[256,1024]{1,0:T(8,128)}, f32[256,1024]{1,0:T(8,128)}, bf16[256,1024]{1,0:T(8,128)(2,1)}) custom-call(f32[256,1024]{1,0:T(8,128)S(1)} %get-tuple-element.12.refs_0_, f32[256,1024]{1,0:T(8,128)S(1)} %bitcast.11, f32[256,1024]{1,0:T(8,128)S(1)} %bitcast.12, bf16[256,1024]{1,0:T(8,128)(2,1)S(1)} %bitcast.13), custom_call_target="tpu_custom_call" | custom-call | tf_op jit(solution)/shard_map/pallas_call | solution.py:487
